TPU v7x, 512 devices: a whole 4x8x8 slice. The times are simulated.
512 devices in a mesh: bunch: 32 (over y, x), tile: 16 (over z, core).
Axes of the slice: x: 4, y: 8, z: 8, core: 2. Of those that a mesh axis runs over, the one named last changes fastest.
Arguments:
- cell_index: int32 [2, 32, 2, 16384], P(None, 'bunch', None, 'tile'), may hold values from 0 to 255
- charges: bfloat16 [2, 32, 16384], P(None, 'bunch', 'tile'), may hold values from 0.5 to 2
- momenta: float32 [2, 32, 2, 16384], P(None, 'bunch', None, 'tile'), may hold values from -6 to 6
- fill_pattern: int32 [2, 32], P(None, 'bunch'), may hold values 0 or 1
- encounters: int32 [4, 2, 2, 32], P(None, None, None, 'bunch'), may hold values 0 or 1
- green_spectrum: float32 [256, 256], P(None, 'tile'), may hold values from 0.5 to 4
- stop_gain: float32 [4], replicated, may hold values from 0.5 to 2
- parasitic_gain: float32 [4], replicated, may hold values from 0.25 to 1
Outputs:
- kicked: float32 [2, 32, 2, 16384], P(None, 'bunch', None, 'tile')
All inputs are finite; a program needn't handle non-finite values. No bound on the sum of `fill_pattern` or of `encounters` on one device may be relied on, other than what follows from the above.
Results may differ from a plain program's by a relative error of at most 0.0037.
Values may be sent and summed in bfloat16 or wider, within the bound.
A program may use at most 128 MiB of HBM per device.

v0:
```python
import math
import jax
import jax.numpy as jnp
from jax import lax
from jax.sharding import PartitionSpec as P

GRID = 256
STOPS = 4
OFFSET_CELLS = 32


def from_behind(value, axis, steps):
    count = lax.axis_size(axis)
    pairs = [(source, (source + steps) % count) for source in range(count)]
    return lax.ppermute(value, axis, pairs)


def tables(grid):
    positions = jnp.arange(grid, dtype=jnp.int32)
    phases = (positions[:, None] * positions[None, :] % grid).astype(jnp.float32) * (
        2.0 * math.pi / grid
    )
    return (jnp.cos(phases), jnp.sin(phases))


def transform(matrix, operand):
    return jnp.einsum("mi,ibn->mbn", matrix, operand, precision=lax.Precision.HIGHEST)


def shifted_up(operand, amount):
    kept = operand[..., : GRID - amount]
    widths = [(0, 0)] * (operand.ndim - 1) + [(amount, 0)]
    return jnp.pad(kept, widths)


def shifted_down(operand, amount):
    kept = operand[..., amount:]
    widths = [(0, 0)] * (operand.ndim - 1) + [(0, amount)]
    return jnp.pad(kept, widths)


def pick_rows(field_b, rows_p, cols_p):
    row_count = field_b.shape[0]
    inside = (rows_p >= 0) & (rows_p < row_count)
    safe_row = jnp.clip(rows_p, 0, row_count - 1)
    values = field_b[safe_row, :, cols_p].astype(jnp.float32)
    return jnp.where(inside[:, None], values, 0.0).T


def encounter_sum(partners, encounter_marks, stop_gain, parasitic_gain):
    summed = jnp.zeros(partners[0].shape, jnp.float32)
    for stop_number in range(STOPS):
        summed = summed + stop_gain[stop_number] * partners[stop_number].astype(jnp.float32)
        weight = stop_gain[stop_number] * parasitic_gain[stop_number]
        mark_up = encounter_marks[stop_number, 0].astype(jnp.float32)[None, :, None, None]
        following = shifted_up(partners[stop_number + 1].astype(jnp.float32), OFFSET_CELLS)
        summed = summed + weight * mark_up * following
        if stop_number >= 1:
            mark_down = encounter_marks[stop_number, 1].astype(jnp.float32)[None, :, None, None]
            earlier = shifted_down(partners[stop_number - 1].astype(jnp.float32), OFFSET_CELLS)
            summed = summed + weight * mark_down * earlier
    return summed.astype(jnp.bfloat16)


def body(
    cell_index,
    charges,
    momenta,
    fill_pattern,
    encounters,
    green_spectrum,
    stop_gain,
    parasitic_gain,
):
    bunches_here = cell_index.shape[1]
    particles = cell_index.shape[3]
    grid_count = 2 * bunches_here
    tile_count = lax.axis_size("tile")
    tile_rows = GRID // tile_count
    row_of = cell_index[:, :, 0].reshape(grid_count, particles)
    col_of = cell_index[:, :, 1].reshape(grid_count, particles)
    masked = (charges * fill_pattern.astype(jnp.bfloat16)[:, :, None]).reshape(
        grid_count, particles
    )
    columns = jnp.arange(GRID, dtype=jnp.int32)
    block_size = min(1024, particles)
    block_count = particles // block_size
    rows_here = jnp.arange(tile_rows * lax.axis_size("tile"), dtype=jnp.int32)

    def deposit_one_grid(operands):
        rows_p, cols_p, weight_p = operands
        blocks = (
            rows_p.reshape(block_count, block_size),
            cols_p.reshape(block_count, block_size),
            weight_p.reshape(block_count, block_size),
        )

        def add_block(running, block):
            rows_b, cols_b, weight_b = block
            left_hot = jnp.where(
                rows_b[:, None] == rows_here[None, :],
                weight_b[:, None],
                jnp.zeros((), jnp.bfloat16),
            )
            right_hot = (cols_b[:, None] == columns[None, :]).astype(jnp.bfloat16)
            return (
                running
                + jnp.einsum("pr,pc->rc", left_hot, right_hot, preferred_element_type=jnp.float32),
                None,
            )

        start = jnp.zeros((tile_rows * lax.axis_size("tile"), GRID), jnp.float32)
        result, unused = lax.scan(add_block, start, blocks)
        return result

    per_grid = lax.map(deposit_one_grid, (row_of, col_of, masked))
    charge = lax.psum_scatter(
        jnp.transpose(per_grid, (1, 0, 2)), "tile", scatter_dimension=0, tiled=True
    )
    cosine_table, sine_table = tables(GRID)
    real_part = jnp.einsum("rbg,gn->rbn", charge, cosine_table, precision=lax.Precision.HIGHEST)
    imag_part = -jnp.einsum("rbg,gn->rbn", charge, sine_table, precision=lax.Precision.HIGHEST)
    halves = jnp.stack([real_part, imag_part], axis=2)
    first_col = lax.axis_index("tile") * tile_rows
    col_wave = jnp.sin(
        2.0
        * math.pi
        / GRID
        * (first_col + jnp.arange(tile_rows, dtype=jnp.int32)).astype(jnp.float32)
    )
    row_wave = jnp.sin(2.0 * math.pi / GRID * jnp.arange(GRID, dtype=jnp.int32).astype(jnp.float32))
    columns_block = lax.all_to_all(halves, "tile", split_axis=3, concat_axis=0, tiled=True)
    real_in = columns_block[:, :, 0]
    imag_in = columns_block[:, :, 1]
    spec_real = transform(cosine_table, real_in) + transform(sine_table, imag_in)
    spec_imag = transform(cosine_table, imag_in) - transform(sine_table, real_in)
    pot_real = green_spectrum[:, None, :] * spec_real
    pot_imag = green_spectrum[:, None, :] * spec_imag
    outputs = []
    for sine_wave in (row_wave[:, None, None], col_wave[None, None, :]):
        even_part = sine_wave * pot_imag
        odd_part = -sine_wave * pot_real
        outputs.append(transform(cosine_table, even_part) - transform(sine_table, odd_part))
        outputs.append(transform(sine_table, even_part) + transform(cosine_table, odd_part))
    stacked = jnp.stack(outputs, axis=2)
    returned = lax.all_to_all(stacked, "tile", split_axis=0, concat_axis=3, tiled=True)
    inverse_norm = 1.0 / (GRID * GRID)
    field_x = (
        jnp.einsum("rbn,nj->rbj", returned[:, :, 0], cosine_table, precision=lax.Precision.HIGHEST)
        - jnp.einsum("rbn,nj->rbj", returned[:, :, 1], sine_table, precision=lax.Precision.HIGHEST)
    ) * inverse_norm
    field_y = (
        jnp.einsum("rbn,nj->rbj", returned[:, :, 2], cosine_table, precision=lax.Precision.HIGHEST)
        - jnp.einsum("rbn,nj->rbj", returned[:, :, 3], sine_table, precision=lax.Precision.HIGHEST)
    ) * inverse_norm
    fields = jnp.stack([field_x, field_y], axis=2).astype(jnp.bfloat16)
    beam_first = fields[:, :bunches_here]
    beam_second = fields[:, bunches_here:]
    from_above = [beam_second]
    from_below = [beam_first]
    moving_second = beam_second
    moving_first = beam_first
    for offset in range(1, STOPS + 1):
        moving_second = from_behind(moving_second, "bunch", -1)
        moving_first = from_behind(moving_first, "bunch", 1)
        from_above.append(moving_second)
        from_below.append(moving_first)
    total_first = encounter_sum(from_above, encounters[:, 0], stop_gain, parasitic_gain)
    total_second = encounter_sum(from_below, encounters[:, 1], stop_gain, parasitic_gain)
    totals = jnp.concatenate([total_first, total_second], axis=1)

    def add_one_grid(operands):
        field_b, rows_p, cols_p = operands
        return pick_rows(field_b, rows_p, cols_p)

    kick_sum = lax.map(
        add_one_grid,
        (
            jnp.transpose(lax.all_gather(totals, "tile", axis=0, tiled=True), (1, 0, 2, 3)),
            row_of,
            col_of,
        ),
    )
    return momenta + kick_sum.reshape(2, bunches_here, 2, particles)


def solution(mesh):
    in_specs = (
        P(None, "bunch", None, "tile"),
        P(None, "bunch", "tile"),
        P(None, "bunch", None, "tile"),
        P(None, "bunch"),
        P(None, None, None, "bunch"),
        P(None, "tile"),
        P(),
        P(),
    )
    out_specs = P(None, "bunch", None, "tile")
    return jax.shard_map(body, mesh=mesh, in_specs=in_specs, out_specs=out_specs, check_vma=False)
```

profile of v0, /device:TPU:1, one launch (start us, length us, event | category | flops | bytes accessed | tf_op | source)
XLA Modules:
  0.0 271.0 jit_solution(11180594290852846728)
XLA Ops:
  12.2 62.1 %reduce-scatter.2.cloned.1.call-done = f32[16,2,256]{2,0,1:T(8,128)} async-done(((f32[256,2,256]{2,0,1:T(8,128)}), f32[16,2,256]{2,0,1:T(8,128)}) %reduce-scatter.2.cloned.1.call-update) | async-done | bytes 32784 | tf_op jit(solution)/shard_map/reduce_scatter | solution.py:117
  74.2 2.0 convolution_bitcast_fusion.1
  76.2 2.0 fusion.17
  79.9 7.4 %all-to-all-start = ((f32[16,1,1024]{2,1,0:T(1,128)}), f32[16,1,1024]{2,1,0:T(1,128)S(1)}, u32[]{:S(2)}, u32[]{:S(2)}) async-start(f32[16,1,1024]{2,1,0:T(1,128)} %reshape.198), calls=%async_computation.1 | async-start | bytes 131072 | tf_op jit(solution)/shard_map/all_to_all | solution.py:132
  87.4 7.7 %all-to-all-done = f32[16,1,1024]{2,1,0:T(1,128)S(1)} async-done(((f32[16,1,1024]{2,1,0:T(1,128)}), f32[16,1,1024]{2,1,0:T(1,128)S(1)}, u32[]{:S(2)}, u32[]{:S(2)}) %all-to-all-start) | async-done | bytes 65568 | tf_op jit(solution)/shard_map/all_to_all | solution.py:132
  114.7 2.1 reshape.200
  116.8 3.5 %all-to-all-start.1 = ((f32[16,1,2048]{2,1,0:T(1,128)}), f32[16,1,2048]{2,1,0:T(1,128)S(1)}, u32[]{:S(2)}, u32[]{:S(2)}) async-start(f32[16,1,2048]{2,1,0:T(1,128)} %reshape.200), calls=%async_computation.2 | async-start | bytes 262144 | tf_op jit(solution)/shard_map/all_to_all | solution.py:146
  122.2 7.2 %all-to-all-done.1 = f32[16,1,2048]{2,1,0:T(1,128)S(1)} async-done(((f32[16,1,2048]{2,1,0:T(1,128)}), f32[16,1,2048]{2,1,0:T(1,128)S(1)}, u32[]{:S(2)}, u32[]{:S(2)}) %all-to-all-start.1) | async-done | bytes 131104 | tf_op jit(solution)/shard_map/all_to_all | solution.py:146
  137.8 6.6 %collective-permute-start = (bf16[16,1,2,256]{3,0,1,2:T(8,128)(2,1)S(1)}, bf16[16,1,2,256]{3,0,1,2:T(8,128)(2,1)S(1)}, u32[]{:S(2)}, u32[]{:S(2)}) collective-permute-start(bf16[16,1,2,256]{3,0,1,2:T(8,128)(2,1)S(1)} %get-tuple-element.186), channel_id=1, source_target_pairs={{0,496},{16,0},{32,16},{48,32},{64,48},{80,64},{96,80},{112,96},{1... | collective-permute-start | bytes 49160 | tf_op jit(solution)/shard_map/ppermute | solution.py:15
  160.6 6.7 %collective-permute-start.1 = (bf16[16,1,2,256]{3,0,1,2:T(8,128)(2,1)S(1)}, bf16[16,1,2,256]{3,0,1,2:T(8,128)(2,1)S(1)}, u32[]{:S(2)}, u32[]{:S(2)}) collective-permute-start(bf16[16,1,2,256]{3,0,1,2:T(8,128)(2,1)S(1)} %collective-permute-done), channel_id=1, source_target_pairs={{0,496},{16,0},{32,16},{48,32},{64,48},{80,64},{96,80},{112,96},{1... | collective-permute-start | bytes 49160 | tf_op jit(solution)/shard_map/ppermute | solution.py:15
  167.4 1.9 collective-permute-start.5
  169.4 6.7 %collective-permute-start.2 = (bf16[16,1,2,256]{3,0,1,2:T(8,128)(2,1)S(1)}, bf16[16,1,2,256]{3,0,1,2:T(8,128)(2,1)S(1)}, u32[]{:S(2)}, u32[]{:S(2)}) collective-permute-start(bf16[16,1,2,256]{3,0,1,2:T(8,128)(2,1)S(1)} %collective-permute-done.1), channel_id=1, source_target_pairs={{0,496},{16,0},{32,16},{48,32},{64,48},{80,64},{96,80},{112,96},{1... | collective-permute-start | bytes 49160 | tf_op jit(solution)/shard_map/ppermute | solution.py:15
  176.1 1.9 collective-permute-start.6
  178.0 6.7 %collective-permute-start.3 = (bf16[16,1,2,256]{3,0,1,2:T(8,128)(2,1)S(1)}, bf16[16,1,2,256]{3,0,1,2:T(8,128)(2,1)S(1)}, u32[]{:S(2)}, u32[]{:S(2)}) collective-permute-start(bf16[16,1,2,256]{3,0,1,2:T(8,128)(2,1)S(1)} %collective-permute-done.2), channel_id=1, source_target_pairs={{0,496},{16,0},{32,16},{48,32},{64,48},{80,64},{96,80},{112,96},{1... | collective-permute-start | bytes 49160 | tf_op jit(solution)/shard_map/ppermute | solution.py:15
  184.8 1.9 collective-permute-start.7
  186.8 2.5 add_convert_fusion.1
  189.2 3.4 %collective-permute-done.7 = bf16[16,1,2,256]{3,0,1,2:T(8,128)(2,1)S(1)} collective-permute-done((bf16[16,1,2,256]{3,0,1,2:T(8,128)(2,1)S(1)}, bf16[16,1,2,256]{3,0,1,2:T(8,128)(2,1)S(1)}, u32[]{:S(2)}, u32[]{:S(2)}) %collective-permute-start.7) | collective-permute-done | bytes 16416 | tf_op jit(solution)/shard_map/ppermute | solution.py:15
  192.6 2.5 add_convert_fusion
  195.1 18.9 %all_gather.3 = bf16[256,2,2,256]{3,0,1,2:T(8,128)(2,1)S(1)} all-gather(bf16[16,2,2,256]{3,0,1,2:T(8,128)(2,1)S(1)} %pad_maximum_fusion.2), channel_id=1, replica_groups=mesh['bunch'=32,'tile'=16] {'tile'}, dimensions={0}, use_global_device_ids=true | all-gather | bytes 557056 | tf_op jit(solution)/shard_map/all_gather | solution.py:179
  214.0 49.5 %while.29 = (s32[]{:T(128)}, f32[2,2,1024]{2,1,0:T(2,128)S(1)}, s32[2,1024]{1,0:T(2,128)S(1)}, bf16[2,256,2,256]{3,1,0,2:T(8,128)(2,1)S(1)}, s32[2,1024]{1,0:T(2,128)S(1)}, /*index=5*/s32[]{:T(128)}) while((s32[]{:T(128)}, f32[2,2,1024]{2,1,0:T(2,128)S(1)}, s32[2,1024]{1,0:T(2,128)S(1)}, bf16[2,256,2,256]{3,1,0,2:T(8,128)(2,1)S(1)}, ...), condition=%wide.region_4.5_spmd, body=%wide.region_3.4_spmd.sunk | while | flops 19458 | bytes 1128533 | solution.py:176
  214.1 11.9 %copy.94 = bf16[1,256,2,256]{2,3,1,0:T(8,128)(2,1)} copy(bf16[1,256,2,256]{3,1,0,2:T(8,128)(2,1)S(1)} %constant_dynamic-slice_fusion.5) | data formatting | bytes 524288 | tf_op jit(solution)/shard_map/while/body/jit(dynamic_index_in_dim)/dynamic_slice | solution.py:176
  226.0 12.3 %gather_fusion = bf16[1024,2]{1,0:T(8,128)(2,1)S(1)} fusion(bf16[256,2,256]{1,2,0:T(8,128)(2,1)} %bitcast.203, s32[1024]{0:T(1024)S(1)} %bitcast.202), kind=kCustom, calls=%fused_computation.clone.1 | custom fusion | bytes 16384 | tf_op jit(solution)/shard_map/while/body/eval_jaxpr/gather | solution.py:46
  238.9 11.9 %copy.94 = bf16[1,256,2,256]{2,3,1,0:T(8,128)(2,1)} copy(bf16[1,256,2,256]{3,1,0,2:T(8,128)(2,1)S(1)} %constant_dynamic-slice_fusion.5) | data formatting | bytes 524288 | tf_op jit(solution)/shard_map/while/body/jit(dynamic_index_in_dim)/dynamic_slice | solution.py:176
  250.8 12.3 %gather_fusion = bf16[1024,2]{1,0:T(8,128)(2,1)S(1)} fusion(bf16[256,2,256]{1,2,0:T(8,128)(2,1)} %bitcast.203, s32[1024]{0:T(1024)S(1)} %bitcast.202), kind=kCustom, calls=%fused_computation.clone.1 | custom fusion | bytes 16384 | tf_op jit(solution)/shard_map/while/body/eval_jaxpr/gather | solution.py:46
  (99 shorter events, 43.4 us)
Async XLA Ops:
  6.5 96.4 %copy-start.1 = (f32[256,16]{0,1:T(8,128)S(1)}, f32[256,16]{0,1:T(8,128)}, u32[]{:S(2)}) copy-start(f32[256,16]{0,1:T(8,128)} %param.17) | copy-start | bytes 49156
  6.5 113.7 %copy-start.3 = (f32[4]{0:T(128)S(1)}, f32[4]{0:T(128)}, u32[]{:S(2)}) copy-start(f32[4]{0:T(128)} %param.18) | copy-start | bytes 52
  6.5 67.7 %reduce-scatter.2.cloned.1.call-start = ((), (), s32[]{:S(2)}) async-start(), calls=%async_computation.3 | async-start | bytes 557056 | tf_op jit(solution)/shard_map/reduce_scatter | solution.py:117
  10.6 0.8 copy-start
  10.6 133.7 %copy-start.4 = (f32[4]{0:T(128)S(1)}, f32[4]{0:T(128)}, u32[]{:S(2)}) copy-start(f32[4]{0:T(128)} %param.19) | copy-start | bytes 52
  79.9 15.2 %all-to-all-start = ((f32[16,1,1024]{2,1,0:T(1,128)}), f32[16,1,1024]{2,1,0:T(1,128)S(1)}, u32[]{:S(2)}, u32[]{:S(2)}) async-start(f32[16,1,1024]{2,1,0:T(1,128)} %reshape.198), calls=%async_computation.1 | async-start | bytes 131072 | tf_op jit(solution)/shard_map/all_to_all | solution.py:132
  116.8 12.7 %all-to-all-start.1 = ((f32[16,1,2048]{2,1,0:T(1,128)}), f32[16,1,2048]{2,1,0:T(1,128)S(1)}, u32[]{:S(2)}, u32[]{:S(2)}) async-start(f32[16,1,2048]{2,1,0:T(1,128)} %reshape.200), calls=%async_computation.2 | async-start | bytes 262144 | tf_op jit(solution)/shard_map/all_to_all | solution.py:146
  137.8 22.8 %collective-permute-start = (bf16[16,1,2,256]{3,0,1,2:T(8,128)(2,1)S(1)}, bf16[16,1,2,256]{3,0,1,2:T(8,128)(2,1)S(1)}, u32[]{:S(2)}, u32[]{:S(2)}) collective-permute-start(bf16[16,1,2,256]{3,0,1,2:T(8,128)(2,1)S(1)} %get-tuple-element.186), channel_id=1, source_target_pairs={{0,496},{16,0},{32,16},{48,32},{64,48},{80,64},{96,80},{112,96},{1... | collective-permute-start | bytes 49160 | tf_op jit(solution)/shard_map/ppermute | solution.py:15
  158.6 8.8 %collective-permute-start.4 = (bf16[16,1,2,256]{3,0,1,2:T(8,128)(2,1)S(1)}, bf16[16,1,2,256]{3,0,1,2:T(8,128)(2,1)S(1)}, u32[]{:S(2)}, u32[]{:S(2)}) collective-permute-start(bf16[16,1,2,256]{3,0,1,2:T(8,128)(2,1)S(1)} %get-tuple-element.187), channel_id=1, source_target_pairs={{0,16},{16,32},{32,48},{48,64},{64,80},{80,96},{96,112},{112,128},... | collective-permute-start | bytes 49160 | tf_op jit(solution)/shard_map/ppermute | solution.py:15
  160.6 8.8 %collective-permute-start.1 = (bf16[16,1,2,256]{3,0,1,2:T(8,128)(2,1)S(1)}, bf16[16,1,2,256]{3,0,1,2:T(8,128)(2,1)S(1)}, u32[]{:S(2)}, u32[]{:S(2)}) collective-permute-start(bf16[16,1,2,256]{3,0,1,2:T(8,128)(2,1)S(1)} %collective-permute-done), channel_id=1, source_target_pairs={{0,496},{16,0},{32,16},{48,32},{64,48},{80,64},{96,80},{112,96},{1... | collective-permute-start | bytes 49160 | tf_op jit(solution)/shard_map/ppermute | solution.py:15
  167.4 8.8 %collective-permute-start.5 = (bf16[16,1,2,256]{3,0,1,2:T(8,128)(2,1)S(1)}, bf16[16,1,2,256]{3,0,1,2:T(8,128)(2,1)S(1)}, u32[]{:S(2)}, u32[]{:S(2)}) collective-permute-start(bf16[16,1,2,256]{3,0,1,2:T(8,128)(2,1)S(1)} %collective-permute-done.4), channel_id=1, source_target_pairs={{0,16},{16,32},{32,48},{48,64},{64,80},{80,96},{96,112},{112,128},... | collective-permute-start | bytes 49160 | tf_op jit(solution)/shard_map/ppermute | solution.py:15
  169.4 8.7 %collective-permute-start.2 = (bf16[16,1,2,256]{3,0,1,2:T(8,128)(2,1)S(1)}, bf16[16,1,2,256]{3,0,1,2:T(8,128)(2,1)S(1)}, u32[]{:S(2)}, u32[]{:S(2)}) collective-permute-start(bf16[16,1,2,256]{3,0,1,2:T(8,128)(2,1)S(1)} %collective-permute-done.1), channel_id=1, source_target_pairs={{0,496},{16,0},{32,16},{48,32},{64,48},{80,64},{96,80},{112,96},{1... | collective-permute-start | bytes 49160 | tf_op jit(solution)/shard_map/ppermute | solution.py:15
  176.1 8.7 %collective-permute-start.6 = (bf16[16,1,2,256]{3,0,1,2:T(8,128)(2,1)S(1)}, bf16[16,1,2,256]{3,0,1,2:T(8,128)(2,1)S(1)}, u32[]{:S(2)}, u32[]{:S(2)}) collective-permute-start(bf16[16,1,2,256]{3,0,1,2:T(8,128)(2,1)S(1)} %collective-permute-done.5), channel_id=1, source_target_pairs={{0,16},{16,32},{32,48},{48,64},{64,80},{80,96},{96,112},{112,128},... | collective-permute-start | bytes 49160 | tf_op jit(solution)/shard_map/ppermute | solution.py:15
  178.0 8.7 %collective-permute-start.3 = (bf16[16,1,2,256]{3,0,1,2:T(8,128)(2,1)S(1)}, bf16[16,1,2,256]{3,0,1,2:T(8,128)(2,1)S(1)}, u32[]{:S(2)}, u32[]{:S(2)}) collective-permute-start(bf16[16,1,2,256]{3,0,1,2:T(8,128)(2,1)S(1)} %collective-permute-done.2), channel_id=1, source_target_pairs={{0,496},{16,0},{32,16},{48,32},{64,48},{80,64},{96,80},{112,96},{1... | collective-permute-start | bytes 49160 | tf_op jit(solution)/shard_map/ppermute | solution.py:15
  184.8 7.8 %collective-permute-start.7 = (bf16[16,1,2,256]{3,0,1,2:T(8,128)(2,1)S(1)}, bf16[16,1,2,256]{3,0,1,2:T(8,128)(2,1)S(1)}, u32[]{:S(2)}, u32[]{:S(2)}) collective-permute-start(bf16[16,1,2,256]{3,0,1,2:T(8,128)(2,1)S(1)} %collective-permute-done.6), channel_id=1, source_target_pairs={{0,16},{16,32},{32,48},{48,64},{64,80},{80,96},{96,112},{112,128},... | collective-permute-start | bytes 49160 | tf_op jit(solution)/shard_map/ppermute | solution.py:15
  214.0 49.5 %copy-start.2 = (f32[2,1,2,1024]{3,2,1,0:T(2,128)S(1)}, f32[2,1,2,1024]{3,2,1,0:T(2,128)}, u32[]{:S(2)}) copy-start(f32[2,1,2,1024]{3,2,1,0:T(2,128)} %param.14) | copy-start | bytes 49156
Sparse Core Ops, SparseCore 0:
  11.6 62.6 reduce-scatter.1
where the time goes:
time: 272 us; the launch traced here: 271 us
  waiting for transfers between devices  80.5 us (30%)
  local copies, waits for them, and re-layouts  63.1 us (23%)
  starting transfers between devices  45.1 us (17%)
  between operations  27.4 us (10%)
  matrix products  26.5 us (10%)
  blocking collectives  18.9 us (7%)
  other arithmetic  9.5 us (3%)
    reduce_scatter x1, waiting for transfers between devices, body(): lax.psum_scatter(jnp.transpose(per_grid, (1, 0, 2)), 'tile', scatter_dime...  62.1 us
    ppermute x8, starting transfers between devices, from_behind(): return lax.ppermute(value, axis, pairs)  34.3 us
    gather x2, local copies, waits for them, and re-layouts, pick_rows(): values = field_b[safe_row, :, cols_p].astype(jnp.float32)  24.6 us
    dynamic_slice x4, local copies, waits for them, and re-layouts, body(): lax.map(add_one_grid, (jnp.transpose(lax.all_gather(totals, 'tile', axis=...  23.9 us
    all_gather x1, blocking collectives, body(): lax.all_gather(totals, 'tile', axis=0, tiled=True)  18.9 us
    unnamed x12, matrix products  16 us
    all_to_all x1, waiting for transfers between devices, body(): lax.all_to_all(halves, 'tile', split_axis=3, concat_axis=0, tiled=True)  7.72 us
    all_to_all x1, starting transfers between devices, body(): lax.all_to_all(halves, 'tile', split_axis=3, concat_axis=0, tiled=True)  7.36 us
  transfers between devices with their start and end apart: 11, of which 4 were waited for; matrix products, arithmetic and copies ran while one was open for 2% of the time, Pallas kernels for 0%

commit v1 on v0

--- a/solution.py
+++ b/solution.py
@@ -176,7 +176,13 @@
     kick_sum = lax.map(
         add_one_grid,
         (
-            jnp.transpose(lax.all_gather(totals, "tile", axis=0, tiled=True), (1, 0, 2, 3)),
+            jnp.transpose(
+                jnp.concatenate(
+                    lax.all_to_all(jnp.stack([totals] * lax.axis_size("tile")), "tile", 0, 0),
+                    axis=0,
+                ),
+                (1, 0, 2, 3),
+            ),
             row_of,
             col_of,
         ),

time: 272 us -> 278 us (1.022)
  blocking collectives: 18.9 us -> 0 us
  waiting for transfers between devices: 80.5 us -> 97.7 us
  starting transfers between devices: 45.1 us -> 51.3 us
    all_gather x1 -> x0, blocking collectives: 18.9 us -> none  [body(): lax.all_gather(totals, 'tile', axis=0, tiled=True)]
    all_to_all x0 -> x1, waiting for transfers between devices: none -> 17.3 us  [body(): lax.all_to_all(jnp.stack([totals] * lax.axis_size('tile')), 'tile', 0, 0)]
    all_to_all x0 -> x1, starting transfers between devices: none -> 6.17 us  [body(): lax.all_to_all(jnp.stack([totals] * lax.axis_size('tile')), 'tile', 0, 0)]
  transfers between devices with their start and end apart: 11 -> 12, of which waited for: 4 -> 5; matrix products, arithmetic and copies ran while one was open for 2% -> 2% of each run, Pallas kernels for 0% -> 0%
where the time goes in v1:
time: 278 us; the launch traced here: 277 us
  waiting for transfers between devices  97.7 us (35%)
  local copies, waits for them, and re-layouts  64.2 us (23%)
  starting transfers between devices  51.3 us (18%)
  between operations  27.4 us (10%)
  matrix products  26.5 us (10%)
  other arithmetic  9.8 us (4%)
    reduce_scatter x1, waiting for transfers between devices, body(): lax.psum_scatter(jnp.transpose(per_grid, (1, 0, 2)), 'tile', scatter_dime...  62.1 us
    ppermute x8, starting transfers between devices, from_behind(): return lax.ppermute(value, axis, pairs)  34.3 us
    gather x2, local copies, waits for them, and re-layouts, pick_rows(): values = field_b[safe_row, :, cols_p].astype(jnp.float32)  24.7 us
    dynamic_slice x4, local copies, waits for them, and re-layouts, body(): lax.map(add_one_grid, (jnp.transpose(jnp.concatenate(lax.all_to_all(jnp.s...  23.9 us
    all_to_all x1, waiting for transfers between devices, body(): lax.all_to_all(jnp.stack([totals] * lax.axis_size('tile')), 'tile', 0, 0)  17.3 us
    unnamed x12, matrix products  16 us
    all_to_all x1, waiting for transfers between devices, body(): lax.all_to_all(halves, 'tile', split_axis=3, concat_axis=0, tiled=True)  7.72 us
    all_to_all x1, starting transfers between devices, body(): lax.all_to_all(halves, 'tile', split_axis=3, concat_axis=0, tiled=True)  7.36 us
  transfers between devices with their start and end apart: 12, of which 5 were waited for; matrix products, arithmetic and copies ran while one was open for 2% of the time, Pallas kernels for 0%

profile of v1, /device:TPU:1, one launch (start us, length us, event | category | flops | bytes accessed | tf_op | source)
XLA Modules:
  0.0 276.9 jit_solution(11179310995289421112)
XLA Ops:
  12.1 62.1 %reduce-scatter.2.cloned.1.call-done = f32[16,2,256]{2,0,1:T(8,128)} async-done(((f32[256,2,256]{2,0,1:T(8,128)}), f32[16,2,256]{2,0,1:T(8,128)}) %reduce-scatter.2.cloned.1.call-update) | async-done | bytes 32784 | tf_op jit(solution)/shard_map/reduce_scatter | solution.py:117
  74.2 2.0 convolution_bitcast_fusion.1
  76.2 2.0 fusion.17
  79.9 7.4 %all-to-all-start = ((f32[16,1,1024]{2,1,0:T(1,128)}), f32[16,1,1024]{2,1,0:T(1,128)S(1)}, u32[]{:S(2)}, u32[]{:S(2)}) async-start(f32[16,1,1024]{2,1,0:T(1,128)} %reshape.204), calls=%async_computation.1 | async-start | bytes 131072 | tf_op jit(solution)/shard_map/all_to_all | solution.py:132
  87.4 7.7 %all-to-all-done = f32[16,1,1024]{2,1,0:T(1,128)S(1)} async-done(((f32[16,1,1024]{2,1,0:T(1,128)}), f32[16,1,1024]{2,1,0:T(1,128)S(1)}, u32[]{:S(2)}, u32[]{:S(2)}) %all-to-all-start) | async-done | bytes 65568 | tf_op jit(solution)/shard_map/all_to_all | solution.py:132
  114.7 2.1 reshape.206
  116.8 3.5 %all-to-all-start.1 = ((f32[16,1,2048]{2,1,0:T(1,128)}), f32[16,1,2048]{2,1,0:T(1,128)S(1)}, u32[]{:S(2)}, u32[]{:S(2)}) async-start(f32[16,1,2048]{2,1,0:T(1,128)} %reshape.206), calls=%async_computation.2 | async-start | bytes 262144 | tf_op jit(solution)/shard_map/all_to_all | solution.py:146
  122.2 7.2 %all-to-all-done.1 = f32[16,1,2048]{2,1,0:T(1,128)S(1)} async-done(((f32[16,1,2048]{2,1,0:T(1,128)}), f32[16,1,2048]{2,1,0:T(1,128)S(1)}, u32[]{:S(2)}, u32[]{:S(2)}) %all-to-all-start.1) | async-done | bytes 131104 | tf_op jit(solution)/shard_map/all_to_all | solution.py:146
  137.8 6.6 %collective-permute-start = (bf16[16,1,2,256]{3,0,1,2:T(8,128)(2,1)S(1)}, bf16[16,1,2,256]{3,0,1,2:T(8,128)(2,1)S(1)}, u32[]{:S(2)}, u32[]{:S(2)}) collective-permute-start(bf16[16,1,2,256]{3,0,1,2:T(8,128)(2,1)S(1)} %get-tuple-element.176), channel_id=1, source_target_pairs={{0,496},{16,0},{32,16},{48,32},{64,48},{80,64},{96,80},{112,96},{1... | collective-permute-start | bytes 49160 | tf_op jit(solution)/shard_map/ppermute | solution.py:15
  160.7 6.7 %collective-permute-start.1 = (bf16[16,1,2,256]{3,0,1,2:T(8,128)(2,1)S(1)}, bf16[16,1,2,256]{3,0,1,2:T(8,128)(2,1)S(1)}, u32[]{:S(2)}, u32[]{:S(2)}) collective-permute-start(bf16[16,1,2,256]{3,0,1,2:T(8,128)(2,1)S(1)} %collective-permute-done), channel_id=1, source_target_pairs={{0,496},{16,0},{32,16},{48,32},{64,48},{80,64},{96,80},{112,96},{1... | collective-permute-start | bytes 49160 | tf_op jit(solution)/shard_map/ppermute | solution.py:15
  167.5 1.9 collective-permute-start.5
  169.5 6.7 %collective-permute-start.2 = (bf16[16,1,2,256]{3,0,1,2:T(8,128)(2,1)S(1)}, bf16[16,1,2,256]{3,0,1,2:T(8,128)(2,1)S(1)}, u32[]{:S(2)}, u32[]{:S(2)}) collective-permute-start(bf16[16,1,2,256]{3,0,1,2:T(8,128)(2,1)S(1)} %collective-permute-done.1), channel_id=1, source_target_pairs={{0,496},{16,0},{32,16},{48,32},{64,48},{80,64},{96,80},{112,96},{1... | collective-permute-start | bytes 49160 | tf_op jit(solution)/shard_map/ppermute | solution.py:15
  178.2 6.7 %collective-permute-start.3 = (bf16[16,1,2,256]{3,0,1,2:T(8,128)(2,1)S(1)}, bf16[16,1,2,256]{3,0,1,2:T(8,128)(2,1)S(1)}, u32[]{:S(2)}, u32[]{:S(2)}) collective-permute-start(bf16[16,1,2,256]{3,0,1,2:T(8,128)(2,1)S(1)} %collective-permute-done.2), channel_id=1, source_target_pairs={{0,496},{16,0},{32,16},{48,32},{64,48},{80,64},{96,80},{112,96},{1... | collective-permute-start | bytes 49160 | tf_op jit(solution)/shard_map/ppermute | solution.py:15
  184.9 1.9 collective-permute-start.7
  186.9 2.6 add_convert_fusion.1
  189.5 3.2 %collective-permute-done.7 = bf16[16,1,2,256]{3,0,1,2:T(8,128)(2,1)S(1)} collective-permute-done((bf16[16,1,2,256]{3,0,1,2:T(8,128)(2,1)S(1)}, bf16[16,1,2,256]{3,0,1,2:T(8,128)(2,1)S(1)}, u32[]{:S(2)}, u32[]{:S(2)}) %collective-permute-start.7) | collective-permute-done | bytes 16416 | tf_op jit(solution)/shard_map/ppermute | solution.py:15
  192.7 2.6 add_convert_fusion
  196.2 6.2 %all-to-all-start.2 = ((bf16[16,16,2,2,256]{4,1,3,2,0:T(8,128)(2,1)}), bf16[16,16,2,2,256]{4,1,3,2,0:T(8,128)(2,1)S(1)}, u32[]{:S(2)}, u32[]{:S(2)}) async-start(bf16[16,16,2,2,256]{4,1,3,2,0:T(8,128)(2,1)} %stack.66), calls=%async_computation.3 | async-start | bytes 1048576 | tf_op jit(solution)/shard_map/all_to_all | solution.py:181
  202.4 17.3 %all-to-all-done.2 = bf16[16,16,2,2,256]{4,1,3,2,0:T(8,128)(2,1)S(1)} async-done(((bf16[16,16,2,2,256]{4,1,3,2,0:T(8,128)(2,1)}), bf16[16,16,2,2,256]{4,1,3,2,0:T(8,128)(2,1)S(1)}, u32[]{:S(2)}, u32[]{:S(2)}) %all-to-all-start.2) | async-done | bytes 524320 | tf_op jit(solution)/shard_map/all_to_all | solution.py:181
  219.8 49.6 %while.29 = (s32[]{:T(128)}, f32[2,2,1024]{2,1,0:T(2,128)S(1)}, s32[2,1024]{1,0:T(2,128)S(1)}, bf16[2,256,2,256]{3,1,2,0:T(8,128)(2,1)S(1)}, s32[2,1024]{1,0:T(2,128)S(1)}, /*index=5*/s32[]{:T(128)}) while((s32[]{:T(128)}, f32[2,2,1024]{2,1,0:T(2,128)S(1)}, s32[2,1024]{1,0:T(2,128)S(1)}, bf16[2,256,2,256]{3,1,2,0:T(8,128)(2,1)S(1)}, ...), condition=%wide.region_4.5_spmd, body=%wide.region_3.4_spmd.sunk | while | flops 19458 | bytes 1128533 | solution.py:176
  219.9 11.9 %copy.114 = bf16[1,256,2,256]{2,3,1,0:T(8,128)(2,1)} copy(bf16[1,256,2,256]{3,1,2,0:T(8,128)(2,1)S(1)} %constant_dynamic-slice_fusion.5) | data formatting | bytes 524288 | tf_op jit(solution)/shard_map/while/body/jit(dynamic_index_in_dim)/dynamic_slice | solution.py:176
  231.9 12.3 %gather_fusion = bf16[1024,2]{1,0:T(8,128)(2,1)S(1)} fusion(bf16[256,2,256]{1,2,0:T(8,128)(2,1)} %bitcast.205, s32[1024]{0:T(1024)S(1)} %bitcast.204), kind=kCustom, calls=%fused_computation.clone.1 | custom fusion | bytes 16384 | tf_op jit(solution)/shard_map/while/body/eval_jaxpr/gather | solution.py:46
  244.7 11.9 %copy.114 = bf16[1,256,2,256]{2,3,1,0:T(8,128)(2,1)} copy(bf16[1,256,2,256]{3,1,2,0:T(8,128)(2,1)S(1)} %constant_dynamic-slice_fusion.5) | data formatting | bytes 524288 | tf_op jit(solution)/shard_map/while/body/jit(dynamic_index_in_dim)/dynamic_slice | solution.py:176
  256.6 12.4 %gather_fusion = bf16[1024,2]{1,0:T(8,128)(2,1)S(1)} fusion(bf16[256,2,256]{1,2,0:T(8,128)(2,1)} %bitcast.205, s32[1024]{0:T(1024)S(1)} %bitcast.204), kind=kCustom, calls=%fused_computation.clone.1 | custom fusion | bytes 16384 | tf_op jit(solution)/shard_map/while/body/eval_jaxpr/gather | solution.py:46
  (103 shorter events, 46.3 us)
Async XLA Ops:
  6.5 96.4 %copy-start.1 = (f32[256,16]{0,1:T(8,128)S(1)}, f32[256,16]{0,1:T(8,128)}, u32[]{:S(2)}) copy-start(f32[256,16]{0,1:T(8,128)} %param.17) | copy-start | bytes 49156
  6.5 113.7 %copy-start.3 = (f32[4]{0:T(128)S(1)}, f32[4]{0:T(128)}, u32[]{:S(2)}) copy-start(f32[4]{0:T(128)} %param.18) | copy-start | bytes 52
  6.5 67.7 %reduce-scatter.2.cloned.1.call-start = ((), (), s32[]{:S(2)}) async-start(), calls=%async_computation.4 | async-start | bytes 557056 | tf_op jit(solution)/shard_map/reduce_scatter | solution.py:117
  10.6 0.8 copy-start
  10.6 133.8 %copy-start.4 = (f32[4]{0:T(128)S(1)}, f32[4]{0:T(128)}, u32[]{:S(2)}) copy-start(f32[4]{0:T(128)} %param.19) | copy-start | bytes 52
  79.9 15.2 %all-to-all-start = ((f32[16,1,1024]{2,1,0:T(1,128)}), f32[16,1,1024]{2,1,0:T(1,128)S(1)}, u32[]{:S(2)}, u32[]{:S(2)}) async-start(f32[16,1,1024]{2,1,0:T(1,128)} %reshape.204), calls=%async_computation.1 | async-start | bytes 131072 | tf_op jit(solution)/shard_map/all_to_all | solution.py:132
  116.8 12.7 %all-to-all-start.1 = ((f32[16,1,2048]{2,1,0:T(1,128)}), f32[16,1,2048]{2,1,0:T(1,128)S(1)}, u32[]{:S(2)}, u32[]{:S(2)}) async-start(f32[16,1,2048]{2,1,0:T(1,128)} %reshape.206), calls=%async_computation.2 | async-start | bytes 262144 | tf_op jit(solution)/shard_map/all_to_all | solution.py:146
  137.8 22.9 %collective-permute-start = (bf16[16,1,2,256]{3,0,1,2:T(8,128)(2,1)S(1)}, bf16[16,1,2,256]{3,0,1,2:T(8,128)(2,1)S(1)}, u32[]{:S(2)}, u32[]{:S(2)}) collective-permute-start(bf16[16,1,2,256]{3,0,1,2:T(8,128)(2,1)S(1)} %get-tuple-element.176), channel_id=1, source_target_pairs={{0,496},{16,0},{32,16},{48,32},{64,48},{80,64},{96,80},{112,96},{1... | collective-permute-start | bytes 49160 | tf_op jit(solution)/shard_map/ppermute | solution.py:15
  158.7 8.8 %collective-permute-start.4 = (bf16[16,1,2,256]{3,0,1,2:T(8,128)(2,1)S(1)}, bf16[16,1,2,256]{3,0,1,2:T(8,128)(2,1)S(1)}, u32[]{:S(2)}, u32[]{:S(2)}) collective-permute-start(bf16[16,1,2,256]{3,0,1,2:T(8,128)(2,1)S(1)} %get-tuple-element.177), channel_id=1, source_target_pairs={{0,16},{16,32},{32,48},{48,64},{64,80},{80,96},{96,112},{112,128},... | collective-permute-start | bytes 49160 | tf_op jit(solution)/shard_map/ppermute | solution.py:15
  160.7 8.8 %collective-permute-start.1 = (bf16[16,1,2,256]{3,0,1,2:T(8,128)(2,1)S(1)}, bf16[16,1,2,256]{3,0,1,2:T(8,128)(2,1)S(1)}, u32[]{:S(2)}, u32[]{:S(2)}) collective-permute-start(bf16[16,1,2,256]{3,0,1,2:T(8,128)(2,1)S(1)} %collective-permute-done), channel_id=1, source_target_pairs={{0,496},{16,0},{32,16},{48,32},{64,48},{80,64},{96,80},{112,96},{1... | collective-permute-start | bytes 49160 | tf_op jit(solution)/shard_map/ppermute | solution.py:15
  167.5 8.8 %collective-permute-start.5 = (bf16[16,1,2,256]{3,0,1,2:T(8,128)(2,1)S(1)}, bf16[16,1,2,256]{3,0,1,2:T(8,128)(2,1)S(1)}, u32[]{:S(2)}, u32[]{:S(2)}) collective-permute-start(bf16[16,1,2,256]{3,0,1,2:T(8,128)(2,1)S(1)} %collective-permute-done.4), channel_id=1, source_target_pairs={{0,16},{16,32},{32,48},{48,64},{64,80},{80,96},{96,112},{112,128},... | collective-permute-start | bytes 49160 | tf_op jit(solution)/shard_map/ppermute | solution.py:15
  169.5 8.7 %collective-permute-start.2 = (bf16[16,1,2,256]{3,0,1,2:T(8,128)(2,1)S(1)}, bf16[16,1,2,256]{3,0,1,2:T(8,128)(2,1)S(1)}, u32[]{:S(2)}, u32[]{:S(2)}) collective-permute-start(bf16[16,1,2,256]{3,0,1,2:T(8,128)(2,1)S(1)} %collective-permute-done.1), channel_id=1, source_target_pairs={{0,496},{16,0},{32,16},{48,32},{64,48},{80,64},{96,80},{112,96},{1... | collective-permute-start | bytes 49160 | tf_op jit(solution)/shard_map/ppermute | solution.py:15
  176.2 8.7 %collective-permute-start.6 = (bf16[16,1,2,256]{3,0,1,2:T(8,128)(2,1)S(1)}, bf16[16,1,2,256]{3,0,1,2:T(8,128)(2,1)S(1)}, u32[]{:S(2)}, u32[]{:S(2)}) collective-permute-start(bf16[16,1,2,256]{3,0,1,2:T(8,128)(2,1)S(1)} %collective-permute-done.5), channel_id=1, source_target_pairs={{0,16},{16,32},{32,48},{48,64},{64,80},{80,96},{96,112},{112,128},... | collective-permute-start | bytes 49160 | tf_op jit(solution)/shard_map/ppermute | solution.py:15
  178.2 8.7 %collective-permute-start.3 = (bf16[16,1,2,256]{3,0,1,2:T(8,128)(2,1)S(1)}, bf16[16,1,2,256]{3,0,1,2:T(8,128)(2,1)S(1)}, u32[]{:S(2)}, u32[]{:S(2)}) collective-permute-start(bf16[16,1,2,256]{3,0,1,2:T(8,128)(2,1)S(1)} %collective-permute-done.2), channel_id=1, source_target_pairs={{0,496},{16,0},{32,16},{48,32},{64,48},{80,64},{96,80},{112,96},{1... | collective-permute-start | bytes 49160 | tf_op jit(solution)/shard_map/ppermute | solution.py:15
  184.9 7.8 %collective-permute-start.7 = (bf16[16,1,2,256]{3,0,1,2:T(8,128)(2,1)S(1)}, bf16[16,1,2,256]{3,0,1,2:T(8,128)(2,1)S(1)}, u32[]{:S(2)}, u32[]{:S(2)}) collective-permute-start(bf16[16,1,2,256]{3,0,1,2:T(8,128)(2,1)S(1)} %collective-permute-done.6), channel_id=1, source_target_pairs={{0,16},{16,32},{32,48},{48,64},{64,80},{80,96},{96,112},{112,128},... | collective-permute-start | bytes 49160 | tf_op jit(solution)/shard_map/ppermute | solution.py:15
  196.2 23.5 %all-to-all-start.2 = ((bf16[16,16,2,2,256]{4,1,3,2,0:T(8,128)(2,1)}), bf16[16,16,2,2,256]{4,1,3,2,0:T(8,128)(2,1)S(1)}, u32[]{:S(2)}, u32[]{:S(2)}) async-start(bf16[16,16,2,2,256]{4,1,3,2,0:T(8,128)(2,1)} %stack.66), calls=%async_computation.3 | async-start | bytes 1048576 | tf_op jit(solution)/shard_map/all_to_all | solution.py:181
  219.8 49.7 %copy-start.2 = (f32[2,1,2,1024]{3,2,1,0:T(2,128)S(1)}, f32[2,1,2,1024]{3,2,1,0:T(2,128)}, u32[]{:S(2)}) copy-start(f32[2,1,2,1024]{3,2,1,0:T(2,128)} %param.14) | copy-start | bytes 49156
Sparse Core Ops, SparseCore 0:
  11.6 62.6 reduce-scatter.1
